TPU v7x, 512 devices: a whole 4x4x16 slice. The times are simulated.
512 devices in a mesh: seq: 64 (over z, y), head: 8 (over x, core).
Axes of the slice: x: 4, y: 4, z: 16, core: 2. Of those that a mesh axis runs over, the one named last changes fastest.
Arguments:
- stream_x: bfloat16 [16384, 3072], P('seq', 'head')
- qkv_weight: bfloat16 [3072, 4608], P(None, 'head')
- short_lengths: int32 [32], replicated, may hold values from 1 to 256, 4096 in all
- cache_owner: int32 [16384, 1], P('seq'), may hold values from 0 to 63, as said below
Outputs:
- attended: bfloat16 [16384, 1536], P('seq', 'head')
- row_lse: float32 [16, 16384], P('head', 'seq')
- kv_cache: bfloat16 [32768, 3072], P('seq', 'head')
Inputs may be any that keep to these rules, and one draw needn't show every extreme that they name: `short_lengths`: the lengths sum to 4096 and the longest is exactly 256. `cache_owner`: the rows of one device form 256 / 8 aligned pages of 8 rows; all rows of a page name the same owner, and the pages of one device name different owners, so an owner takes either none or exactly 8 rows of one device.
All inputs are finite; a program needn't handle non-finite values.
Results may differ from a plain program's by a relative error of at most 0.0083.
Values may be sent and summed in bfloat16 or wider, within the bound.
No kernel may reach another device: no remote copies, remote signals or barrier semaphores. Data moves between devices by JAX's collectives and lax.ppermute only.
A program may use at most 128 MiB of HBM per device.

v0:
```python
import math
import jax
import jax.numpy as jnp
from jax import lax
from jax.sharding import PartitionSpec as P

HD = 96
neg_large = -1e30
rope_base = 10000.0


def boundaries(short_lengths, long_length):
    running = jnp.cumsum(short_lengths)
    return jnp.concatenate([jnp.zeros((1,), jnp.int32), running]) + long_length


def locate(row_ids, bounds):
    passed = row_ids[:, None] >= bounds[None, :]
    segment = jnp.sum(passed.astype(jnp.int32), axis=1)
    seg_begin = jnp.max(jnp.where(passed, bounds[None, :], 0), axis=1)
    return (segment, seg_begin)


def rotate(parts, position, head_dim):
    half_dim = head_dim // 2
    inverse_freq = rope_base ** (-jnp.arange(half_dim, dtype=jnp.float32) / half_dim)
    angle = position[:, None, None] * inverse_freq[None, None, :]
    cosine = jnp.cos(angle)
    sine_part = jnp.sin(angle)
    first_half = parts[..., :half_dim]
    second_half = parts[..., half_dim:]
    return jnp.concatenate(
        [
            first_half * cosine - second_half * sine_part,
            second_half * cosine + first_half * sine_part,
        ],
        axis=-1,
    )


def body(stream_x, qkv_weight, short_lengths, cache_owner):
    seq_count = lax.axis_size("seq")
    tok_count = stream_x.shape[0]
    heads_here = qkv_weight.shape[1] // (3 * HD)
    long_length = tok_count * (seq_count * 11 // 16)
    bounds = boundaries(short_lengths, long_length)
    pad_segment = short_lengths.shape[0] + 1
    first_row = lax.axis_index("seq") * tok_count
    row_ids = first_row + jnp.arange(tok_count, dtype=jnp.int32)
    segment, seg_begin = locate(row_ids, bounds)
    position = (row_ids - seg_begin).astype(jnp.float32)
    is_padding = segment == pad_segment
    projected = jnp.dot(
        lax.all_gather(stream_x, "head", axis=1, tiled=True),
        qkv_weight,
        preferred_element_type=jnp.float32,
    )
    projected = projected.reshape(tok_count, heads_here, 3, HD)
    queries = rotate(projected[:, :, 0], position, HD).astype(jnp.bfloat16)
    rotated_keys = rotate(projected[:, :, 1], position, HD).astype(jnp.bfloat16)
    values = projected[:, :, 2].astype(jnp.bfloat16)
    packed = jnp.stack([rotated_keys, values], axis=2).reshape(tok_count, heads_here * 2 * HD)
    score_scale = 1.0 / math.sqrt(HD)
    shard_piece = lax.all_gather(packed, "seq", axis=0, tiled=True)
    key_count = shard_piece.shape[0]
    key_ids = jnp.arange(key_count, dtype=jnp.int32)
    row_max = jnp.full((heads_here, tok_count), neg_large, jnp.float32)
    key_segment, unused = locate(key_ids, bounds)
    key_value = shard_piece.reshape(key_count, heads_here, 2, HD)
    scores = (
        jnp.einsum("qhe,khe->hqk", queries, key_value[:, :, 0], preferred_element_type=jnp.float32)
        * score_scale
    )
    allowed = (
        (key_segment[None, :] == segment[:, None])
        & (key_ids[None, :] <= row_ids[:, None])
        & (key_ids[None, :] >= 0)
    )
    new_max = jnp.maximum(row_max, jnp.max(jnp.where(allowed[None], scores, neg_large), axis=2))
    weights = jnp.where(allowed[None], jnp.exp(scores - new_max[:, :, None]), 0.0)
    denominator = jnp.sum(weights, axis=2)
    context = jnp.einsum(
        "hqk,khe->hqe",
        weights.astype(jnp.bfloat16),
        key_value[:, :, 1],
        preferred_element_type=jnp.float32,
    )
    running = (new_max, denominator, context)
    row_max, denominator, context = running
    context = context / denominator[:, :, None]
    row_lse = jnp.where(is_padding[None, :], 0.0, row_max + jnp.log(denominator))
    context = jnp.where(is_padding[None, :, None], 0.0, context)
    attended = (
        jnp.transpose(context, (1, 0, 2)).reshape(tok_count, heads_here * HD).astype(jnp.bfloat16)
    )
    capacity = 2 * tok_count // seq_count
    owner_ids = cache_owner[:, 0]
    one_hot = (owner_ids[:, None] == jnp.arange(seq_count, dtype=jnp.int32)[None, :]).astype(
        jnp.int32
    )
    owner_rank = jnp.sum(jnp.cumsum(one_hot, axis=0) * one_hot, axis=1) - 1
    slot_index = owner_ids * capacity + owner_rank
    cached = jnp.where(is_padding[:, None], jnp.zeros_like(packed), packed)
    outbox = (
        jnp.zeros((seq_count * capacity, packed.shape[1]), jnp.bfloat16).at[slot_index].set(cached)
    )
    received = lax.all_to_all(
        outbox.reshape(seq_count, capacity, packed.shape[1]),
        "seq",
        split_axis=0,
        concat_axis=0,
        tiled=True,
    )
    kv_cache = received.reshape(seq_count * capacity, packed.shape[1])
    return (attended, row_lse, kv_cache)


def solution(mesh):
    return jax.shard_map(
        body,
        mesh=mesh,
        in_specs=(P("seq", "head"), P(None, "head"), P(), P("seq", None)),
        out_specs=(P("seq", "head"), P("head", "seq"), P("seq", "head")),
        check_vma=False,
    )
```

profile of v0, /device:TPU:32, one launch (start us, length us, event | category | flops | bytes accessed | tf_op | source)
XLA Modules:
  0.0 311.0 jit_solution(13779810520924512798)
XLA Ops:
  7.2 0.0 copy-start
  7.2 0.0 all-gather.3.cloned.1.call-start
  7.2 0.7 all-gather.3.cloned.1.call-update
  7.9 0.0 all-gather.5.cloned.1.call-start
  8.0 1.6 copy.28
  9.6 0.8 reduce-window.18
  10.3 0.6 reduce
  11.0 0.7 add_add_fusion
  11.7 0.0 copy-start.1
  11.7 0.1 fusion.29
  11.8 0.4 copy-done.1
  12.2 0.9 multiply_cosine_fusion
  13.1 33.3 %all-gather.3.cloned.1.call-done = bf16[256,3072]{1,0:T(8,128)(2,1)} async-done(((bf16[256,384]{1,0:T(8,128)(2,1)}), bf16[256,3072]{1,0:T(8,128)(2,1)}) %all-gather.3.cloned.1.call-update) | async-done | bytes 1572880 | tf_op jit(solution)/shard_map/all_gather | solution.py:54
  46.4 0.0 copy-done
  46.5 2.5 fusion.35
  49.0 1.5 subtract_convert_fusion.1
  50.6 0.7 copy.32
  51.3 0.0 all-gather.5.cloned.1.call-update
  51.3 1.3 fusion.26
  52.6 2.0 reduce-window.19
  54.6 1.0 slice_reduce_fusion
  55.6 1.0 fusion.25
  56.6 1.7 convert_reduce_fusion
  58.3 0.7 compare_select_fusion.1
  59.0 1.6 broadcast_select_fusion
  60.7 1.7 copy.36
  62.4 2.6 scatter_custom_fusion
  65.0 15.8 %all-to-all-start = ((bf16[64,8,384]{2,1,0:T(8,128)(2,1)}), bf16[64,8,384]{2,1,0:T(8,128)(2,1)}, u32[]{:S(2)}, u32[]{:S(2)}) async-start(bf16[64,8,384]{2,1,0:T(8,128)(2,1)} %bitcast.67), calls=%async_computation | async-start | bytes 786432 | tf_op jit(solution)/shard_map/all_to_all | solution.py:107
  80.9 8.0 %fusion.4 = pred[256,16384]{1,0:T(8,128)(4,1)} fusion(s32[256]{0:T(256)S(1)} %iota_add_fusion, s32[16384]{0:T(1024)} %convert_reduce_fusion, s32[256]{0:T(256)S(1)} %get-tuple-element.3), kind=kLoop, calls=%fused_computation.7 | loop fusion | flops 12582912 | bytes 4261888 | tf_op jit(solution)/shard_map/and | solution.py:75
  88.9 21.2 %all-to-all-done = bf16[64,8,384]{2,1,0:T(8,128)(2,1)} async-done(((bf16[64,8,384]{2,1,0:T(8,128)(2,1)}), bf16[64,8,384]{2,1,0:T(8,128)(2,1)}, u32[]{:S(2)}, u32[]{:S(2)}) %all-to-all-start) | async-done | bytes 393248 | tf_op jit(solution)/shard_map/all_to_all | solution.py:107
  110.1 141.5 %all-gather.5.cloned.1.call-done = bf16[16384,384]{0,1:T(8,128)(2,1)} async-done(((bf16[256,384]{0,1:T(8,128)(2,1)}), bf16[16384,384]{0,1:T(8,128)(2,1)}) %all-gather.5.cloned.1.call-update) | async-done | bytes 12582928 | tf_op jit(solution)/shard_map/all_gather | solution.py:64
  251.6 17.4 %select_reduce_fusion = (f32[2,256]{1,0:T(2,128)S(1)}, f32[2,256,16384]{2,1,0:T(8,128)}) fusion(pred[256,16384]{1,0:T(8,128)(4,1)} %fusion.4, bf16[16384,2,2,96]{0,3,2,1:T(8,128)(2,1)} %bitcast.76, bf16[256,2,48]{0,2,1:T(8,128)(2,1)} %get-tuple-element.8, bf16[256,2,48]{0,2,1:T(8,128)(2,1)} %get-tuple-element.7), kind=kOutput, calls=%fused_computation.2 | convolution fusion | flops 1635974656 | bytes 44140544 | tf_op jit(solution)/shard_map/qhe,khe->hqk/dot_general | solution.py:71
  269.0 15.9 %fusion = f32[2,256]{1,0:T(2,128)S(1)} fusion(f32[2,256,16384]{2,1,0:T(8,128)} %get-tuple-element.16, f32[2,256]{1,0:T(2,128)S(1)} %broadcast_maximum_fusion, pred[256,16384]{1,0:T(8,128)(4,1)} %fusion.4), kind=kLoop, calls=%fused_computation.3 | loop fusion | flops 33553920 | bytes 37752832 | tf_op jit(solution)/shard_map/reduce_sum | solution.py:81
  284.8 0.6 add_select_fusion
  285.4 16.9 %fusion.16 = bf16[256,2,96]{0,2,1:T(8,128)(2,1)} fusion(bf16[16384,2,2,96]{0,3,2,1:T(8,128)(2,1)} %bitcast.77, f32[2,256,16384]{2,1,0:T(8,128)} %get-tuple-element.16, f32[2,256]{1,0:T(2,128)S(1)} %broadcast_maximum_fusion, pred[256,16384]{1,0:T(8,128)(4,1)} %fusion.4, f32[256,2]{0,1:T(2,128)S(1)} %bitcast.72, pred[256]{0:T(512)(128)(4,1)S(1)} %broadcast_compare_fusion), kind=kOutput, calls=%fused_computation.17 | convolution fusion | flops 1644314624 | bytes 44142848 | tf_op jit(solution)/shard_map/hqk,khe->hqe/dot_general | solution.py:82
  302.4 1.8 copy.51
  (11 shorter events, 0.2 us)
Async XLA Ops:
  7.2 39.3 %copy-start = (bf16[3072,576]{0,1:T(8,128)(2,1)S(1)}, bf16[3072,576]{0,1:T(8,128)(2,1)}, u32[]{:S(2)}) copy-start(bf16[3072,576]{0,1:T(8,128)(2,1)} %param.5) | copy-start | bytes 10616836
  7.2 39.3 %all-gather.3.cloned.1.call-start = ((), (), s32[]{:S(2)}) async-start(), calls=%async_computation.1 | async-start | bytes 1769472 | tf_op jit(solution)/shard_map/all_gather | solution.py:54
  7.9 243.7 %all-gather.5.cloned.1.call-start = ((), (), s32[]{:S(2)}) async-start(), calls=%async_computation.2 | async-start | bytes 12779520 | tf_op jit(solution)/shard_map/all_gather | solution.py:64
  11.7 0.5 copy-start.1
  65.0 45.1 %all-to-all-start = ((bf16[64,8,384]{2,1,0:T(8,128)(2,1)}), bf16[64,8,384]{2,1,0:T(8,128)(2,1)}, u32[]{:S(2)}, u32[]{:S(2)}) async-start(bf16[64,8,384]{2,1,0:T(8,128)(2,1)} %bitcast.67), calls=%async_computation | async-start | bytes 786432 | tf_op jit(solution)/shard_map/all_to_all | solution.py:107
Sparse Core Ops, SparseCore 0:
  10.1 36.2 all-gather.2
  51.4 200.1 all-gather.4
where the time goes:
time: 312 us; the launch traced here: 311 us
  waiting for transfers between devices  197 us (63%)
  other arithmetic  37.5 us (12%)
  matrix products  36.8 us (12%)
  starting transfers between devices  15.9 us (5%)
  between operations  14.1 us (5%)
  local copies, waits for them, and re-layouts  9.93 us (3%)
    all_gather x1, waiting for transfers between devices, body(): shard_piece = lax.all_gather(packed, 'seq', axis=0, tiled=True)  142 us
    all_gather x1, waiting for transfers between devices, body(): lax.all_gather(stream_x, 'head', axis=1, tiled=True)  33.3 us
    all_to_all x1, waiting for transfers between devices, body(): lax.all_to_all(outbox.reshape(seq_count, capacity, packed.shape[1]), 'seq...  21.2 us
    dot_general x1, matrix products, body(): jnp.einsum('qhe,khe->hqk', queries, key_value[:, :, 0], preferred_element...  17.4 us
    dot_general x1, matrix products, body(): jnp.einsum('hqk,khe->hqe', weights.astype(jnp.bfloat16), key_value[:, :,...  16.9 us
    reduce_sum x1, other arithmetic, body(): denominator = jnp.sum(weights, axis=2)  15.9 us
    all_to_all x1, starting transfers between devices, body(): lax.all_to_all(outbox.reshape(seq_count, capacity, packed.shape[1]), 'seq...  15.8 us
    and x1, other arithmetic, body(): (key_segment[None, :] == segment[:, None]) & (key_ids[None, :] <= row_ids...  8.02 us
  transfers between devices with their start and end apart: 3, of which 3 were waited for; matrix products, arithmetic and copies ran while one was open for 9% of the time, Pallas kernels for 0%

commit v1 on v0

--- a/solution.py
+++ b/solution.py
@@ -61,7 +61,9 @@
     values = projected[:, :, 2].astype(jnp.bfloat16)
     packed = jnp.stack([rotated_keys, values], axis=2).reshape(tok_count, heads_here * 2 * HD)
     score_scale = 1.0 / math.sqrt(HD)
-    shard_piece = lax.all_gather(packed, "seq", axis=0, tiled=True)
+    shard_piece = jnp.concatenate(
+        lax.all_to_all(jnp.stack([packed] * lax.axis_size("seq")), "seq", 0, 0), axis=0
+    )
     key_count = shard_piece.shape[0]
     key_ids = jnp.arange(key_count, dtype=jnp.int32)
     row_max = jnp.full((heads_here, tok_count), neg_large, jnp.float32)

time: 312 us -> 751 us (2.41)
  the two profiles are of different devices: /device:TPU:32 before, /device:TPU:8 now
where the time goes in v1:
time: 751 us; the launch traced here: 750 us
  waiting for transfers between devices  569 us (76%)
  local copies, waits for them, and re-layouts  44.9 us (6%)
  blocking collectives  43.1 us (6%)
  matrix products  38.8 us (5%)
  other arithmetic  33.7 us (4%)
  between operations  14.2 us (2%)
    all_to_all x1, waiting for transfers between devices, body(): lax.all_to_all(jnp.stack([packed] * lax.axis_size('seq')), 'seq', 0, 0)  541 us
    all_to_all x1, blocking collectives, body(): lax.all_to_all(outbox.reshape(seq_count, capacity, packed.shape[1]), 'seq...  43.1 us
    all_gather x1, waiting for transfers between devices, body(): lax.all_gather(stream_x, 'head', axis=1, tiled=True)  27.4 us
    another operation x1, local copies, waits for them, and re-layouts, body(): key_value = shard_piece.reshape(key_count, heads_here, 2, HD)  19.5 us
    dot_general x1, matrix products, body(): jnp.einsum('qhe,khe->hqk', queries, key_value[:, :, 0], preferred_element...  18.5 us
    dot_general x1, matrix products, body(): jnp.einsum('hqk,khe->hqe', weights.astype(jnp.bfloat16), key_value[:, :,...  17.8 us
    reduce_sum x1, other arithmetic, body(): denominator = jnp.sum(weights, axis=2)  15.9 us
  transfers between devices with their start and end apart: 2, of which 2 were waited for; matrix products, arithmetic and copies ran while one was open for 3% of the time, Pallas kernels for 0%

profile of v1, /device:TPU:8, one launch (start us, length us, event | category | flops | bytes accessed | tf_op | source)
XLA Modules:
  0.0 750.1 jit_solution(1783660177433897865)
XLA Ops:
  7.2 0.0 copy-start
  7.2 0.0 all-gather.2.cloned.1.call-start
  7.2 0.7 all-gather.2.cloned.1.call-update
  7.9 1.7 copy.38
  9.6 0.8 reduce-window.18
  10.3 0.6 reduce
  11.0 1.3 fusion.26
  12.3 2.0 reduce-window.19
  14.3 1.0 slice_reduce_fusion
  15.3 0.7 add_add_fusion
  16.1 0.1 fusion.29
  16.2 0.9 fusion.25
  17.2 1.2 compare_select_fusion.1
  18.4 0.9 multiply_cosine_fusion
  19.3 27.4 %all-gather.2.cloned.1.call-done = bf16[256,3072]{1,0:T(8,128)(2,1)} async-done(((bf16[256,384]{1,0:T(8,128)(2,1)}), bf16[256,3072]{1,0:T(8,128)(2,1)}) %all-gather.2.cloned.1.call-update) | async-done | bytes 1572880 | tf_op jit(solution)/shard_map/all_gather | solution.py:54
  46.7 0.0 copy-done
  46.7 2.5 fusion.35
  49.3 0.9 subtract_convert_fusion.1
  50.3 0.2 copy.47
  50.5 1.7 scatter_custom_fusion
  52.2 43.1 %all_to_all.10 = bf16[64,8,384]{2,1,0:T(8,128)(2,1)} all-to-all(bf16[64,8,384]{2,1,0:T(8,128)(2,1)S(1)} %bitcast.69), channel_id=1, replica_groups=mesh['seq'=64,'head'=8] {'seq'}, dimensions={0} | all-to-all | bytes 786432 | tf_op jit(solution)/shard_map/all_to_all | solution.py:109
  95.3 6.0 stack.9
  101.3 6.1 all-to-all-start
  107.5 0.5 convert_reduce_fusion
  107.9 7.2 fusion.4
  115.1 541.2 %all-to-all-done = bf16[64,256,384]{1,2,0:T(8,128)(2,1)} async-done(((bf16[64,256,384]{1,2,0:T(8,128)(2,1)}), bf16[64,256,384]{1,2,0:T(8,128)(2,1)}, u32[]{:S(2)}, u32[]{:S(2)}) %all-to-all-start) | async-done | bytes 12582944 | tf_op jit(solution)/shard_map/all_to_all | solution.py:65
  656.3 14.0 %copy.43 = bf16[64,256,384]{1,0,2:T(8,128)(2,1)} copy(bf16[64,256,384]{1,2,0:T(8,128)(2,1)} %all-to-all-done) | data formatting | bytes 25165824 | tf_op jit(solution)/shard_map/all_to_all | solution.py:65
  670.3 19.5 %reshape_reshape.3 = bf16[16384,2,2,96]{0,3,2,1:T(8,128)(2,1)} reshape(bf16[64,256,384]{1,0,2:T(8,128)(2,1)} %copy.43) | data formatting | bytes 25165824 | tf_op jit(solution)/shard_map/reshape;reshape | solution.py:71
  689.8 18.5 %select_reduce_fusion = (f32[2,256]{1,0:T(2,128)S(1)}, f32[2,256,16384]{2,1,0:T(8,128)}) fusion(pred[256,16384]{1,0:T(8,128)(4,1)} %fusion.4, bf16[16384,2,2,96]{0,3,2,1:T(8,128)(2,1)} %reshape_reshape.3, bf16[256,2,48]{0,2,1:T(8,128)(2,1)S(1)} %get-tuple-element.8, bf16[256,2,48]{0,2,1:T(8,128)(2,1)S(1)} %get-tuple-element.7), kind=kOutput, calls=%fused_computation.2 | convolution fusion | flops 1635974656 | bytes 44140544 | tf_op jit(solution)/shard_map/qhe,khe->hqk/dot_general | solution.py:73
  708.3 15.9 %fusion = f32[2,256]{1,0:T(2,128)S(1)} fusion(f32[2,256,16384]{2,1,0:T(8,128)} %get-tuple-element.16, f32[2,256]{1,0:T(2,128)S(1)} %broadcast_maximum_fusion, pred[256,16384]{1,0:T(8,128)(4,1)} %fusion.4), kind=kLoop, calls=%fused_computation.3 | loop fusion | flops 33553920 | bytes 37752832 | tf_op jit(solution)/shard_map/reduce_sum | solution.py:83
  724.2 0.6 add_select_fusion
  724.8 0.0 copy-start.2
  724.8 0.0 copy-start.1
  724.8 17.8 %fusion.16 = bf16[256,2,96]{0,2,1:T(8,128)(2,1)} fusion(bf16[16384,2,2,96]{0,3,2,1:T(8,128)(2,1)} %reshape_reshape.3, f32[2,256,16384]{2,1,0:T(8,128)} %get-tuple-element.16, f32[2,256]{1,0:T(2,128)S(1)} %broadcast_maximum_fusion, pred[256,16384]{1,0:T(8,128)(4,1)} %fusion.4, f32[256,2]{0,1:T(2,128)S(1)} %bitcast.74, ...), kind=kOutput, calls=%fused_computation.17 | convolution fusion | flops 1644314624 | bytes 44142848 | tf_op jit(solution)/shard_map/hqk,khe->hqe/dot_general | solution.py:84
  742.5 0.0 copy-done.2
  742.5 0.7 copy.62
  743.3 0.0 copy-done.1
  (13 shorter events, 0.2 us)
Async XLA Ops:
  7.2 39.6 %copy-start = (bf16[3072,576]{0,1:T(8,128)(2,1)S(1)}, bf16[3072,576]{0,1:T(8,128)(2,1)}, u32[]{:S(2)}) copy-start(bf16[3072,576]{0,1:T(8,128)(2,1)} %param.5) | copy-start | bytes 10616836
  7.2 39.5 %all-gather.2.cloned.1.call-start = ((), (), s32[]{:S(2)}) async-start(), calls=%async_computation.2 | async-start | bytes 1769472 | tf_op jit(solution)/shard_map/all_gather | solution.py:54
  101.3 555.0 %all-to-all-start = ((bf16[64,256,384]{1,2,0:T(8,128)(2,1)}), bf16[64,256,384]{1,2,0:T(8,128)(2,1)}, u32[]{:S(2)}, u32[]{:S(2)}) async-start(bf16[64,256,384]{1,2,0:T(8,128)(2,1)} %stack.9), calls=%async_computation | async-start | bytes 25165824 | tf_op jit(solution)/shard_map/all_to_all | solution.py:65
  724.8 17.8 %copy-start.2 = (bf16[64,8,384]{2,1,0:T(8,128)(2,1)S(1)}, bf16[64,8,384]{2,1,0:T(8,128)(2,1)}, u32[]{:S(2)}) copy-start(bf16[64,8,384]{2,1,0:T(8,128)(2,1)} %all_to_all.10) | copy-start | bytes 1179652
  724.8 18.5 %copy-start.1 = (bf16[3072,576]{0,1:T(8,128)(2,1)S(1)}, bf16[3072,576]{0,1:T(8,128)(2,1)}, u32[]{:S(2)}) copy-start(bf16[3072,576]{0,1:T(8,128)(2,1)} %param.5) | copy-start | bytes 10616836
Sparse Core Ops, SparseCore 0:
  10.1 36.5 all-gather.1
